TPU v7x, 256 devices: a whole 4x4x8 slice. The times are simulated.
256 devices in a mesh: dp: 8 (over x, z_lo), seq: 32 (over z_hi, y, core).
Axes of the slice: x: 4, y: 4, z: 8 (z_hi: 4, z_lo: 2; z = z_hi * 2 + z_lo), core: 2. Of those that a mesh axis runs over, the one named last changes fastest.
Arguments:
- tower_grad: bfloat16 [8192, 768], P(None, ('dp', 'seq')), may hold values from -6 to 6
- act_mid: bfloat16 [16384, 704], P('seq'), may hold values from -6 to 6
- pre_mid: bfloat16 [16384, 768], P('seq', 'dp'), may hold values from -6 to 6
- act_low: bfloat16 [32768, 640], P('seq'), may hold values from -6 to 6
- pre_low: bfloat16 [32768, 704], P('seq', 'dp'), may hold values from -6 to 6
- weight_upper: bfloat16 [5, 704, 768], P(None, 'seq', 'dp'), may hold values from -0.109375 to 0.109375
- weight_lower: bfloat16 [5, 640, 704], P(None, 'seq', 'dp'), may hold values from -0.109375 to 0.109375
Outputs:
- grad_low_act: bfloat16 [32768, 640], P('seq', 'dp')
- grad_upper: float32 [5, 704, 768], P(None, 'seq', 'dp')
- grad_lower: float32 [5, 640, 704], P(None, 'seq', 'dp')
All inputs are finite; a program needn't handle non-finite values.
Results may differ from a plain program's by a relative error of at most 0.0065.
Values may be sent and summed in bfloat16 or wider, within the bound.
No kernel may reach another device: no remote copies, remote signals or barrier semaphores. Data moves between devices by JAX's collectives and lax.ppermute only.
A program may use at most 64 MiB of HBM per device.

v0:
```python
import math
import jax
import jax.numpy as jnp
from jax import lax
from jax.sharding import PartitionSpec as P

KWIDTH = 5


def with_halo(block, sides, width):
    for axis, dim in sides:
        count = lax.axis_size(axis)
        forward = [(i, i + 1) for i in range(count - 1)]
        backward = [(target, source) for source, target in forward]
        low = lax.ppermute(
            lax.slice_in_dim(block, block.shape[dim] - width, None, axis=dim), axis, forward
        )
        high = lax.ppermute(lax.slice_in_dim(block, 0, width, axis=dim), axis, backward)
        block = jnp.concatenate([low, block, high], axis=dim)
    return block


def gelu_slope(pre_act):
    values = pre_act.astype(jnp.float32)
    cumulative = 0.5 * (1.0 + lax.erf(values * (1.0 / math.sqrt(2.0))))
    density = jnp.exp(-0.5 * values * values) * (1.0 / math.sqrt(2.0 * math.pi))
    return cumulative + values * density


def level_back(upper_grad, act, pre_act, weight):
    rows = act.shape[0]
    half = KWIDTH // 2
    spread = jnp.repeat(upper_grad.astype(jnp.float32), 2, axis=0) * 0.5
    pre_grad = (spread * gelu_slope(pre_act)).astype(jnp.bfloat16)
    padded = with_halo(pre_grad, (("seq", 0),), half)
    act_grad = jnp.zeros((rows, weight.shape[1]), jnp.float32)
    pieces = []
    for offset in range(KWIDTH):
        begin = 2 * half - offset
        shifted = padded[begin : begin + rows]
        pieces.append(jnp.einsum("si,so->io", act, shifted, preferred_element_type=jnp.float32))
        act_grad = act_grad + jnp.einsum(
            "so,io->si", shifted, weight[offset], preferred_element_type=jnp.float32
        )
    return (act_grad, jnp.stack(pieces))


def local(tower_grad, act_mid, pre_mid, act_low, pre_low, weight_upper, weight_lower):
    upper_full, lower_full = (
        lax.all_gather(weight_upper, "seq", axis=1, tiled=True),
        lax.all_gather(weight_lower, "seq", axis=1, tiled=True),
    )
    slab_grad = lax.all_to_all(tower_grad, "seq", split_axis=0, concat_axis=1, tiled=True)
    mid_part, upper_part = level_back(slab_grad, act_mid, pre_mid, upper_full)
    mid_total = act_mid.shape[0] * lax.axis_size("seq")
    low_total = act_low.shape[0] * lax.axis_size("seq")
    upper_term = upper_part * (1.0 / math.sqrt(mid_total))
    mid_summed = lax.psum(mid_part, "dp")
    share_width = pre_low.shape[1]
    mid_own = lax.dynamic_slice_in_dim(
        mid_summed, lax.axis_index("dp") * share_width, share_width, 1
    )
    low_part, lower_part = level_back(mid_own.astype(jnp.bfloat16), act_low, pre_low, lower_full)
    lower_term = lower_part * (1.0 / math.sqrt(low_total))
    grad_upper, grad_lower = (
        lax.psum_scatter(upper_term, "seq", scatter_dimension=1, tiled=True),
        lax.psum_scatter(lower_term, "seq", scatter_dimension=1, tiled=True),
    )
    low_grad = lax.psum_scatter(low_part, "dp", scatter_dimension=1, tiled=True)
    return (low_grad.astype(jnp.bfloat16), grad_upper, grad_lower)


def solution(mesh):
    in_specs = (
        P(None, ("dp", "seq")),
        P("seq", None),
        P("seq", "dp"),
        P("seq", None),
        P("seq", "dp"),
        P(None, "seq", "dp"),
        P(None, "seq", "dp"),
    )
    out_specs = (P("seq", "dp"), P(None, "seq", "dp"), P(None, "seq", "dp"))
    return jax.shard_map(local, mesh=mesh, in_specs=in_specs, out_specs=out_specs, check_vma=False)
```

profile of v0, /device:TPU:1, one launch (start us, length us, event | category | flops | bytes accessed | tf_op | source)
XLA Modules:
  0.0 443.1 jit_solution(7031288359553033006)
XLA Ops:
  7.2 13.0 %all-to-all-start = ((bf16[32,256,3]{1,2,0:T(4,128)(2,1)}), bf16[32,256,3]{1,2,0:T(4,128)(2,1)}, u32[]{:S(2)}, u32[]{:S(2)}) async-start(bf16[32,256,3]{1,2,0:T(4,128)(2,1)} %bitcast.113), calls=%async_computation | async-start | bytes 131072 | tf_op jit(solution)/shard_map/all_to_all | solution.py:53
  20.2 0.8 copy.33
  21.0 50.7 %all_gather.6 = bf16[5,704,96]{2,0,1:T(8,128)(2,1)S(1)} all-gather(bf16[5,22,96]{2,0,1:T(8,128)(2,1)S(1)} %copy.33), channel_id=1, replica_groups=mesh['dp'=8,'seq'=32] {'seq'}, dimensions={1}, use_global_device_ids=true | all-gather | bytes 696960 | tf_op jit(solution)/shard_map/all_gather | solution.py:50
  71.7 1.3 fusion.66
  73.0 0.8 copy.32
  73.8 1.1 copy.40
  74.9 0.8 copy.54
  75.7 0.8 copy.53
  76.5 0.8 copy.52
  77.3 0.8 copy.51
  78.1 0.8 copy.55
  78.9 0.9 multiply_bitcast_fusion
  80.2 2.1 collective-permute-start
  82.3 3.5 collective-permute-start.1
  85.8 0.4 fusion.35
  86.5 0.4 fusion.32
  86.9 0.4 fusion.37
  87.4 0.4 fusion.1
  87.8 0.4 fusion
  88.2 68.9 %all-reduce.1 = bf16[512,704]{0,1:T(8,128)(2,1)} all-reduce(f32[512,704]{0,1:T(8,128)S(1)} %fusion), channel_id=1, replica_groups=mesh['dp'=8,'seq'=32] {'dp'}, use_global_device_ids=true, to_apply=%region_0.0 | all-reduce | flops 360448 | bytes 2162688 | tf_op jit(solution)/shard_map/psum | solution.py:58
  157.2 0.9 convert_multiply_fusion.8
  158.7 10.5 %collective-permute-start.2 = (bf16[2,88]{1,0:T(2,128)(2,1)S(1)}, bf16[2,88]{1,0:T(2,128)(2,1)S(1)}, u32[]{:S(2)}, u32[]{:S(2)}) collective-permute-start(bf16[2,88]{1,0:T(2,128)(2,1)S(1)} %get-tuple-element.25), channel_id=1, source_target_pairs={{1,0},{2,1},{3,2},{4,3},{5,4},{6,5},{7,6},{8,7},{9,8},{10,9},{11,1... | collective-permute-start | bytes 1064 | tf_op jit(solution)/shard_map/ppermute | solution.py:18
  169.2 4.2 collective-permute-start.3
  173.4 0.4 fusion.11
  173.8 0.4 fusion.10
  174.2 0.4 fusion.9
  174.5 0.4 fusion.8
  174.9 0.4 fusion.7
  175.4 2.2 copy.48
  177.7 48.1 %all_gather.7 = bf16[5,640,88]{2,0,1:T(8,128)(2,1)} all-gather(bf16[5,20,88]{2,0,1:T(8,128)(2,1)S(1)} %copy.41), channel_id=1, replica_groups=mesh['dp'=8,'seq'=32] {'seq'}, dimensions={1}, use_global_device_ids=true | all-gather | bytes 580800 | tf_op jit(solution)/shard_map/all_gather | solution.py:51
  227.3 0.4 fusion.2
  227.8 2.2 copy.47
  230.2 1.2 copy-done.2
  231.5 2.1 fusion.67
  233.6 1.1 copy.60
  234.7 1.1 copy.59
  235.9 1.1 copy.58
  237.4 0.6 fusion.45
  237.9 0.5 fusion.43
  238.5 0.5 fusion.30
  239.0 0.5 fusion.48
  239.6 2.2 add_add_fusion
  241.8 30.1 %reduce-scatter.8.cloned.1.call-done = f32[5,20,88]{2,0,1:T(8,128)} async-done(((f32[5,640,88]{2,0,1:T(8,128)}), f32[5,20,88]{2,0,1:T(8,128)}) %reduce-scatter.8.cloned.1.call-update) | async-done | bytes 35216 | tf_op jit(solution)/shard_map/reduce_scatter | solution.py:67
  271.9 1.5 copy.50
  273.5 95.1 %reduce-scatter.6.cloned.1.call-done = f32[5,22,96]{2,0,1:T(8,128)} async-done(((f32[5,704,96]{2,0,1:T(8,128)}), f32[5,22,96]{2,0,1:T(8,128)}) %reduce-scatter.6.cloned.1.call-update) | async-done | bytes 42256 | tf_op jit(solution)/shard_map/reduce_scatter | solution.py:66
  368.5 1.5 copy.49
  370.1 64.8 %reduce-scatter.4.cloned.1.call-done = f32[1024,80]{0,1:T(8,128)} async-done(((f32[1024,640]{0,1:T(8,128)}), f32[1024,80]{0,1:T(8,128)}) %reduce-scatter.4.cloned.1.call-update) | async-done | bytes 327696 | tf_op jit(solution)/shard_map/reduce_scatter | solution.py:69
  434.9 1.7 convert_element_type.33
  (48 shorter events, 3.8 us)
Async XLA Ops:
  7.2 166.2 %copy-start = (bf16[1024,640]{1,0:T(8,128)(2,1)S(1)}, bf16[1024,640]{1,0:T(8,128)(2,1)}, u32[]{:S(2)}) copy-start(bf16[1024,640]{1,0:T(8,128)(2,1)} %param.10) | copy-start | bytes 3932164
  7.2 71.8 %all-to-all-start = ((bf16[32,256,3]{1,2,0:T(4,128)(2,1)}), bf16[32,256,3]{1,2,0:T(4,128)(2,1)}, u32[]{:S(2)}, u32[]{:S(2)}) async-start(bf16[32,256,3]{1,2,0:T(4,128)(2,1)} %bitcast.113), calls=%async_computation | async-start | bytes 131072 | tf_op jit(solution)/shard_map/all_to_all | solution.py:53
  20.1 251.8 %reduce-scatter.8.cloned.1.call-start = ((), (), s32[]{:S(2)}) async-start(), calls=%async_computation.6 | async-start | bytes 2703360 | tf_op jit(solution)/shard_map/reduce_scatter | solution.py:67
  71.7 1.3 copy-start.4
  75.7 4.4 copy-start.3
  80.2 6.7 %collective-permute-start = (bf16[2,96]{1,0:T(2,128)(2,1)S(1)}, bf16[2,96]{1,0:T(2,128)(2,1)S(1)}, u32[]{:S(2)}, u32[]{:S(2)}) collective-permute-start(bf16[2,96]{1,0:T(2,128)(2,1)S(1)} %get-tuple-element.27), channel_id=1, source_target_pairs={{1,0},{2,1},{3,2},{4,3},{5,4},{6,5},{7,6},{8,7},{9,8},{10,9},{11,1... | collective-permute-start | bytes 1160 | tf_op jit(solution)/shard_map/ppermute | solution.py:18
  82.3 4.2 collective-permute-start.1
  86.5 1.3 copy-start.6
  86.9 0.5 copy-start.8
  157.2 12.0 %copy-start.5 = (bf16[5,20,88]{2,1,0:T(8,128)(2,1)S(1)}, bf16[5,20,88]{2,1,0:T(8,128)(2,1)}, u32[]{:S(2)}) copy-start(bf16[5,20,88]{2,1,0:T(8,128)(2,1)} %param.13) | copy-start | bytes 52804
  158.7 14.7 %collective-permute-start.2 = (bf16[2,88]{1,0:T(2,128)(2,1)S(1)}, bf16[2,88]{1,0:T(2,128)(2,1)S(1)}, u32[]{:S(2)}, u32[]{:S(2)}) collective-permute-start(bf16[2,88]{1,0:T(2,128)(2,1)S(1)} %get-tuple-element.25), channel_id=1, source_target_pairs={{1,0},{2,1},{3,2},{4,3},{5,4},{6,5},{7,6},{8,7},{9,8},{10,9},{11,1... | collective-permute-start | bytes 1064 | tf_op jit(solution)/shard_map/ppermute | solution.py:18
  169.2 5.4 %collective-permute-start.3 = (bf16[2,88]{1,0:T(2,128)(2,1)S(1)}, bf16[2,88]{1,0:T(2,128)(2,1)S(1)}, u32[]{:S(2)}, u32[]{:S(2)}) collective-permute-start(bf16[2,88]{1,0:T(2,128)(2,1)S(1)} %get-tuple-element.26), channel_id=1, source_target_pairs={{0,1},{1,2},{2,3},{3,4},{4,5},{5,6},{6,7},{7,8},{8,9},{9,10},{10,1... | collective-permute-start | bytes 1064 | tf_op jit(solution)/shard_map/ppermute | solution.py:15
  177.6 48.2 %copy-start.1 = (bf16[512,704]{0,1:T(8,128)(2,1)S(1)}, bf16[512,704]{0,1:T(8,128)(2,1)}, u32[]{:S(2)}) copy-start(bf16[512,704]{0,1:T(8,128)(2,1)} %param.8) | copy-start | bytes 2162692
  177.6 48.2 %copy-start.9 = (bf16[2,96]{1,0:T(2,128)(2,1)S(1)}, bf16[2,96]{1,0:T(2,128)(2,1)}, u32[]{:S(2)}) copy-start(bf16[2,96]{1,0:T(2,128)(2,1)} %copy-done.8) | copy-start | bytes 1156
  177.6 190.9 %reduce-scatter.6.cloned.1.call-start = ((), (), s32[]{:S(2)}) async-start(), calls=%async_computation.5 | async-start | bytes 2973696 | tf_op jit(solution)/shard_map/reduce_scatter | solution.py:66
  225.8 1.1 copy-start.7
  230.0 1.5 copy-start.2
  230.0 204.9 %reduce-scatter.4.cloned.1.call-start = ((), (), s32[]{:S(2)}) async-start(), calls=%async_computation.4 | async-start | bytes 2949120 | tf_op jit(solution)/shard_map/reduce_scatter | solution.py:69
Sparse Core Ops, SparseCore 0:
  177.7 94.1 reduce-scatter.7
  276.3 92.1 reduce-scatter.5
  371.1 63.7 reduce-scatter.3
where the time goes:
time: 444 us; the launch traced here: 443 us
  waiting for transfers between devices  190 us (43%)
  blocking collectives  168 us (38%)
  starting transfers between devices  33.5 us (8%)
  local copies, waits for them, and re-layouts  23.2 us (5%)
  between operations  14.2 us (3%)
  matrix products  10 us (2%)
    reduce_scatter x1, waiting for transfers between devices, local(): lax.psum_scatter(upper_term, 'seq', scatter_dimension=1, tiled=True)  95.1 us
    psum x1, blocking collectives, local(): mid_summed = lax.psum(mid_part, 'dp')  68.9 us
    reduce_scatter x1, waiting for transfers between devices, local(): low_grad = lax.psum_scatter(low_part, 'dp', scatter_dimension=1, tiled=True)  64.8 us
    all_gather x1, blocking collectives, local(): lax.all_gather(weight_upper, 'seq', axis=1, tiled=True)  50.7 us
    all_gather x1, blocking collectives, local(): lax.all_gather(weight_lower, 'seq', axis=1, tiled=True)  48.1 us
    reduce_scatter x1, waiting for transfers between devices, local(): lax.psum_scatter(lower_term, 'seq', scatter_dimension=1, tiled=True)  30.1 us
    unnamed x36, local copies, waits for them, and re-layouts  14.8 us
    all_to_all x1, starting transfers between devices, local(): lax.all_to_all(tower_grad, 'seq', split_axis=0, concat_axis=1, tiled=True)  13 us
  transfers between devices with their start and end apart: 8, of which 4 were waited for; matrix products, arithmetic and copies ran while one was open for 6% of the time, Pallas kernels for 0%

commit v1 on v0

--- a/solution.py
+++ b/solution.py
@@ -55,7 +55,8 @@
     mid_total = act_mid.shape[0] * lax.axis_size("seq")
     low_total = act_low.shape[0] * lax.axis_size("seq")
     upper_term = upper_part * (1.0 / math.sqrt(mid_total))
-    mid_summed = lax.psum(mid_part, "dp")
+    shards = lax.all_gather(mid_part, "dp")
+    mid_summed = jnp.sum(shards, axis=0)
     share_width = pre_low.shape[1]
     mid_own = lax.dynamic_slice_in_dim(
         mid_summed, lax.axis_index("dp") * share_width, share_width, 1

time: 444 us -> 551 us (1.24)
  waiting for transfers between devices: 190 us -> 347 us
  blocking collectives: 168 us -> 99.1 us
  local copies, waits for them, and re-layouts: 23.2 us -> 43.1 us
  starting transfers between devices: 33.5 us -> 24.4 us
  other arithmetic: 4.06 us -> 9.6 us
    all_gather x0 -> x1, waiting for transfers between devices: none -> 190 us  [local(): shards = lax.all_gather(mid_part, 'dp')]
    reduce_scatter x1, waiting for transfers between devices: 95.1 us -> 0.03 us  [local(): lax.psum_scatter(upper_term, 'seq', scatter_dimension=1, tiled=True)]
    psum x1 -> x0, blocking collectives: 68.9 us -> none  [local(): mid_summed = lax.psum(mid_part, 'dp')]
    reduce_scatter x1, waiting for transfers between devices: 30.1 us -> 91 us  [local(): lax.psum_scatter(lower_term, 'seq', scatter_dimension=1, tiled=True)]
    unnamed x36 -> x37, local copies, waits for them, and re-layouts: 14.8 us -> 34.9 us
    ppermute x2, starting transfers between devices: 12.5 us -> 4.65 us  [with_halo(): lax.ppermute(lax.slice_in_dim(block, 0, width, axis=dim), axis, backward)]
    reduce_sum x0 -> x1, other arithmetic: none -> 7.27 us  [local(): mid_summed = jnp.sum(shards, axis=0)]
  transfers between devices with their start and end apart: 8 -> 9, of which waited for: 4 -> 4; matrix products, arithmetic and copies ran while one was open for 6% -> 10% of each run, Pallas kernels for 0% -> 0%
where the time goes in v1:
time: 551 us; the launch traced here: 550 us
  waiting for transfers between devices  347 us (63%)
  blocking collectives  99.1 us (18%)
  local copies, waits for them, and re-layouts  43.1 us (8%)
  starting transfers between devices  24.4 us (4%)
  between operations  16 us (3%)
  matrix products  11.2 us (2%)
  other arithmetic  9.6 us (2%)
    all_gather x1, waiting for transfers between devices, local(): shards = lax.all_gather(mid_part, 'dp')  190 us
    reduce_scatter x1, waiting for transfers between devices, local(): lax.psum_scatter(lower_term, 'seq', scatter_dimension=1, tiled=True)  91 us
    reduce_scatter x1, waiting for transfers between devices, local(): low_grad = lax.psum_scatter(low_part, 'dp', scatter_dimension=1, tiled=True)  64.8 us
    all_gather x1, blocking collectives, local(): lax.all_gather(weight_upper, 'seq', axis=1, tiled=True)  50.8 us
    all_gather x1, blocking collectives, local(): lax.all_gather(weight_lower, 'seq', axis=1, tiled=True)  48.3 us
    unnamed x37, local copies, waits for them, and re-layouts  34.9 us
    all_to_all x1, starting transfers between devices, local(): lax.all_to_all(tower_grad, 'seq', split_axis=0, concat_axis=1, tiled=True)  12.9 us
  transfers between devices with their start and end apart: 9, of which 4 were waited for; matrix products, arithmetic and copies ran while one was open for 10% of the time, Pallas kernels for 0%

profile of v1, /device:TPU:1, one launch (start us, length us, event | category | flops | bytes accessed | tf_op | source)
XLA Modules:
  0.0 550.2 jit_solution(16734197547740259835)
XLA Ops:
  8.0 12.9 %all-to-all-start = ((bf16[32,256,3]{1,2,0:T(4,128)(2,1)}), bf16[32,256,3]{1,2,0:T(4,128)(2,1)S(1)}, u32[]{:S(2)}, u32[]{:S(2)}) async-start(bf16[32,256,3]{1,2,0:T(4,128)(2,1)} %bitcast.119), calls=%async_computation | async-start | bytes 131072 | tf_op jit(solution)/shard_map/all_to_all | solution.py:53
  21.0 0.8 copy.32
  21.7 50.8 %all_gather.12 = bf16[5,704,96]{2,0,1:T(8,128)(2,1)S(1)} all-gather(bf16[5,22,96]{2,0,1:T(8,128)(2,1)S(1)} %copy.32), channel_id=1, replica_groups=mesh['dp'=8,'seq'=32] {'seq'}, dimensions={1}, use_global_device_ids=true | all-gather | bytes 696960 | tf_op jit(solution)/shard_map/all_gather | solution.py:50
  72.6 1.3 fusion.66
  74.0 0.8 copy.51
  74.8 0.8 copy.52
  75.6 0.8 copy.50
  76.4 0.8 copy.54
  77.2 0.8 copy.53
  78.5 2.1 collective-permute-start
  80.6 0.4 fusion.35
  81.0 3.5 collective-permute-start.1
  84.5 0.4 fusion.37
  85.2 0.4 fusion.32
  85.6 0.4 fusion.1
  86.0 1.6 fusion
  87.6 0.8 copy-done.7
  88.4 0.8 copy.39
  89.3 48.3 %all_gather.15 = bf16[5,640,88]{2,0,1:T(8,128)(2,1)S(1)} all-gather(bf16[5,20,88]{2,0,1:T(8,128)(2,1)S(1)} %copy.40), channel_id=1, replica_groups=mesh['dp'=8,'seq'=32] {'seq'}, dimensions={1}, use_global_device_ids=true | all-gather | bytes 580800 | tf_op jit(solution)/shard_map/all_gather | solution.py:51
  137.6 2.0 fusion.67
  139.7 1.8 copy.56
  141.4 0.8 copy.55
  143.3 0.4 fusion.3
  143.7 0.4 fusion.2
  144.2 2.2 copy.46
  146.7 190.5 %all-gather.3.cloned.1.call-done = f32[4096,704]{0,1:T(8,128)} async-done(((f32[512,704]{0,1:T(8,128)}), f32[4096,704]{0,1:T(8,128)}) %all-gather.3.cloned.1.call-update) | async-done | bytes 11534352 | tf_op jit(solution)/shard_map/all_gather | solution.py:58
  337.2 19.9 %copy.60 = f32[88,8,8,512]{3,2,1,0:T(8,128)} copy(f32[88,8,8,512]{3,1,2,0:T(8,128)} %bitcast.116) | data formatting | bytes 23068672
  357.1 7.3 %bitcast_reduce_fusion = bf16[512,704]{0,1:T(8,128)(2,1)S(1)} fusion(f32[88,8,8,512]{3,2,1,0:T(8,128)} %copy.60), kind=kLoop, calls=%fused_computation | loop fusion | flops 2523136 | bytes 12255232 | tf_op jit(solution)/shard_map/reduce_sum | solution.py:59
  364.8 0.6 copy-done.3
  365.6 2.6 collective-permute-start.2
  368.4 0.8 copy.58
  369.3 3.0 collective-permute-start.3
  372.4 0.4 fusion.11
  372.7 0.4 fusion.10
  373.1 0.4 fusion.9
  373.5 0.4 fusion.8
  373.9 0.4 fusion.7
  374.4 2.1 copy.47
  376.6 0.5 fusion.45
  377.4 0.5 fusion.30
  378.3 0.5 fusion.48
  379.2 0.5 fusion.43
  379.8 2.3 add_add_fusion
  382.1 1.5 copy.48
  383.6 91.0 %reduce-scatter.8.cloned.1.call-done = f32[5,20,88]{2,0,1:T(8,128)} async-done(((f32[5,640,88]{2,0,1:T(8,128)}), f32[5,20,88]{2,0,1:T(8,128)}) %reduce-scatter.8.cloned.1.call-update) | async-done | bytes 35216 | tf_op jit(solution)/shard_map/reduce_scatter | solution.py:68
  474.7 1.5 copy.49
  476.2 64.8 %reduce-scatter.4.cloned.1.call-done = f32[1024,80]{0,1:T(8,128)} async-done(((f32[1024,640]{0,1:T(8,128)}), f32[1024,80]{0,1:T(8,128)}) %reduce-scatter.4.cloned.1.call-update) | async-done | bytes 327696 | tf_op jit(solution)/shard_map/reduce_scatter | solution.py:70
  541.0 1.7 convert_element_type.33
  (52 shorter events, 4.5 us)
Async XLA Ops:
  8.0 364.4 %copy-start = (bf16[1024,640]{1,0:T(8,128)(2,1)S(1)}, bf16[1024,640]{1,0:T(8,128)(2,1)}, u32[]{:S(2)}) copy-start(bf16[1024,640]{1,0:T(8,128)(2,1)} %param.10) | copy-start | bytes 3932164
  8.0 70.0 %all-to-all-start = ((bf16[32,256,3]{1,2,0:T(4,128)(2,1)}), bf16[32,256,3]{1,2,0:T(4,128)(2,1)S(1)}, u32[]{:S(2)}, u32[]{:S(2)}) async-start(bf16[32,256,3]{1,2,0:T(4,128)(2,1)} %bitcast.119), calls=%async_computation | async-start | bytes 131072 | tf_op jit(solution)/shard_map/all_to_all | solution.py:53
  20.9 316.3 %all-gather.3.cloned.1.call-start = ((), (), s32[]{:S(2)}) async-start(), calls=%async_computation.7 | async-start | bytes 12976128 | tf_op jit(solution)/shard_map/all_gather | solution.py:58
  72.6 1.3 copy-start.8
  78.5 6.0 %collective-permute-start = (bf16[2,96]{1,0:T(2,128)(2,1)S(1)}, bf16[2,96]{1,0:T(2,128)(2,1)S(1)}, u32[]{:S(2)}, u32[]{:S(2)}) collective-permute-start(bf16[2,96]{1,0:T(2,128)(2,1)S(1)} %get-tuple-element.27), channel_id=1, source_target_pairs={{1,0},{2,1},{3,2},{4,3},{5,4},{6,5},{7,6},{8,7},{9,8},{10,9},{11,1... | collective-permute-start | bytes 1160 | tf_op jit(solution)/shard_map/ppermute | solution.py:18
  81.0 4.2 collective-permute-start.1
  87.5 0.9 copy-start.7
  87.5 1.8 copy-start.9
  87.5 294.5 %reduce-scatter.6.cloned.1.call-start = ((), (), s32[]{:S(2)}) async-start(), calls=%async_computation.5 | async-start | bytes 2973696 | tf_op jit(solution)/shard_map/reduce_scatter | solution.py:67
  137.6 4.6 copy-start.1
  146.5 328.2 %reduce-scatter.8.cloned.1.call-start = ((), (), s32[]{:S(2)}) async-start(), calls=%async_computation.6 | async-start | bytes 2703360 | tf_op jit(solution)/shard_map/reduce_scatter | solution.py:68
  364.4 1.0 copy-start.3
  364.4 3.8 copy-start.2
  365.6 6.7 %collective-permute-start.2 = (bf16[2,88]{1,0:T(2,128)(2,1)S(1)}, bf16[2,88]{1,0:T(2,128)(2,1)S(1)}, u32[]{:S(2)}, u32[]{:S(2)}) collective-permute-start(bf16[2,88]{1,0:T(2,128)(2,1)S(1)} %get-tuple-element.25), channel_id=1, source_target_pairs={{1,0},{2,1},{3,2},{4,3},{5,4},{6,5},{7,6},{8,7},{9,8},{10,9},{11,1... | collective-permute-start | bytes 1064 | tf_op jit(solution)/shard_map/ppermute | solution.py:18
  369.3 4.1 collective-permute-start.3
  376.5 0.9 copy-start.4
  376.5 164.5 %reduce-scatter.4.cloned.1.call-start = ((), (), s32[]{:S(2)}) async-start(), calls=%async_computation.4 | async-start | bytes 2949120 | tf_op jit(solution)/shard_map/reduce_scatter | solution.py:70
  377.4 0.9 copy-start.5
  378.3 0.9 copy-start.6
Sparse Core Ops, SparseCore 0:
  87.7 249.4 all-gather.2
Sparse Core Ops, SparseCore 1:
  146.6 205.3 reduce-scatter.5
  376.6 98.0 reduce-scatter.7
  477.1 63.8 reduce-scatter.3
